TPU v7x, 256 devices: a whole 4x4x8 slice. The times are simulated.
256 devices in a mesh: dp: 8 (over x, core), tm: 32 (over z, y).
Axes of the slice: x: 4, y: 4, z: 8, core: 2. Of those that a mesh axis runs over, the one named last changes fastest.
Arguments:
- latents: bfloat16 [8, 17, 64, 64, 256], P('dp', None, 'tm'), may hold values from -6 to 6
- cotangent: bfloat16 [8, 17, 64, 64, 256], P('dp', None, 'tm'), may hold values from -6 to 6
- spatial_weight: bfloat16 [3, 3, 256, 256], replicated, may hold values from -0.125 to 0.125
- temporal_weight: bfloat16 [3, 256, 256], replicated, may hold values from -0.21875 to 0.21875
Outputs:
- block_out: bfloat16 [8, 17, 64, 64, 256], P('dp', None, 'tm')
- latents_grad: bfloat16 [8, 17, 64, 64, 256], P('dp', None, 'tm')
- spatial_grad: float32 [3, 3, 256, 256], replicated
- temporal_grad: float32 [3, 256, 256], replicated
All inputs are finite; a program needn't handle non-finite values.
Results may differ from a plain program's by a relative error of at most 0.0085.
Values may be sent and summed in bfloat16 or wider, within the bound.
A program may use at most 64 MiB of HBM per device.

v0:
```python
import jax
import jax.numpy as jnp
from jax import lax
from jax.sharding import PartitionSpec as P


def with_halo(cells, sides, width):
    for axis, dim in sides:
        count = lax.axis_size(axis)
        ends = count - 1
        head = lax.slice_in_dim(cells, 0, width, axis=dim)
        tail = lax.slice_in_dim(cells, cells.shape[dim] - width, cells.shape[dim], axis=dim)
        cells = jnp.concatenate(
            [
                lax.ppermute(tail, axis, [(i, (i + 1) % count) for i in range(ends)]),
                cells,
                lax.ppermute(head, axis, [((i + 1) % count, i) for i in range(ends)]),
            ],
            axis=dim,
        )
    return cells


def band_patches(extended, rows_out, flipped):
    padded = jnp.pad(extended, ((0, 0), (0, 0), (1, 1), (0, 0)))
    cols = extended.shape[2]
    pieces = []
    for first in range(3):
        for second in range(3):
            top = 2 - first if flipped else first
            left = 2 - second if flipped else second
            pieces.append(padded[:, top : top + rows_out, left : left + cols, :])
    return jnp.concatenate(pieces, axis=3).reshape(-1, 9 * extended.shape[3])


def causal_mix(act, weight):
    clips, frames, cells, chans = act.shape
    padded = jnp.pad(act, ((0, 0), (2, 0), (0, 0), (0, 0)))
    total = jnp.zeros((clips * frames * cells, chans), jnp.float32)
    for tap in range(3):
        earlier = padded[:, 2 - tap : 2 - tap + frames].reshape(-1, chans)
        total = total + jnp.dot(earlier, weight[tap], preferred_element_type=jnp.float32)
    return total.astype(jnp.bfloat16)


def anti_mix(cot, weight):
    clips, frames, cells, chans = cot.shape
    padded = jnp.pad(cot, ((0, 0), (0, 2), (0, 0), (0, 0)))
    total = jnp.zeros((clips * frames * cells, chans), jnp.float32)
    for tap in range(3):
        later = padded[:, tap : tap + frames].reshape(-1, chans)
        total = total + lax.dot_general(
            later, weight[tap], (((1,), (1,)), ((), ())), preferred_element_type=jnp.float32
        )
    return total.astype(jnp.bfloat16)


def tap_grads(act, cot):
    clips, frames, cells, chans = act.shape
    padded = jnp.pad(act, ((0, 0), (2, 0), (0, 0), (0, 0)))
    cot_flat = cot.reshape(-1, chans)
    parts = []
    for tap in range(3):
        earlier = padded[:, 2 - tap : 2 - tap + frames].reshape(-1, chans)
        parts.append(
            lax.dot_general(
                earlier, cot_flat, (((0,), (0,)), ((), ())), preferred_element_type=jnp.float32
            )
        )
    return jnp.stack(parts)


def silu_grad(act_grad, pre):
    sig = jax.nn.sigmoid(pre)
    return (act_grad.astype(jnp.float32) * sig * (1.0 + pre * (1.0 - sig))).astype(jnp.bfloat16)


def body(latents, cotangent, spatial_weight, temporal_weight):
    clips, frames, rows, cols, chans = latents.shape
    flat_w = spatial_weight.reshape(9 * chans, chans)
    flip_w = jnp.transpose(spatial_weight, (0, 1, 3, 2)).reshape(9 * chans, chans)
    cot_band = cotangent.reshape(clips, frames, rows * cols, chans)
    extended = with_halo(latents, (("tm", 2),), 1)
    patches = band_patches(extended.reshape(clips * frames, rows + 2, cols, chans), rows, False)
    pre = jnp.dot(patches, flat_w, preferred_element_type=jnp.float32)
    act = jax.nn.silu(pre).astype(jnp.bfloat16).reshape(clips, frames, rows * cols, chans)
    mixed = causal_mix(act, temporal_weight)
    act_grad = anti_mix(cot_band, temporal_weight)
    pre_grad = silu_grad(act_grad, pre)
    grad_ext = with_halo(pre_grad.reshape(clips, frames, rows, cols, chans), (("tm", 2),), 1)
    back = jnp.dot(
        band_patches(grad_ext.reshape(clips * frames, rows + 2, cols, chans), rows, True),
        flip_w,
        preferred_element_type=jnp.float32,
    )
    temporal_local = tap_grads(act, cot_band)
    block_out = (latents.reshape(-1, chans).astype(jnp.float32) + mixed.astype(jnp.float32)).astype(
        jnp.bfloat16
    )
    latents_grad = (cotangent.reshape(-1, chans).astype(jnp.float32) + back).astype(jnp.bfloat16)
    spatial_local = lax.dot_general(
        patches, pre_grad, (((0,), (0,)), ((), ())), preferred_element_type=jnp.float32
    )
    spatial_sum, temporal_sum = lax.psum((spatial_local, temporal_local), ("dp", "tm"))
    scale = (clips * lax.axis_size("dp") * frames * rows * lax.axis_size("tm") * cols) ** (-0.5)
    return (
        block_out.reshape(latents.shape),
        latents_grad.reshape(latents.shape),
        (spatial_sum * scale).reshape(3, 3, chans, chans),
        temporal_sum * scale,
    )


def solution(mesh):
    in_specs = (P("dp", None, "tm", None, None), P("dp", None, "tm", None, None), P(), P())
    out_specs = (P("dp", None, "tm", None, None), P("dp", None, "tm", None, None), P(), P())
    return jax.shard_map(body, mesh=mesh, in_specs=in_specs, out_specs=out_specs, check_vma=False)
```

profile of v0, /device:TPU:2, one launch (start us, length us, event | category | flops | bytes accessed | tf_op | source)
XLA Modules:
  0.0 338.0 jit_solution(11071545228273672446)
XLA Ops:
  7.2 2.4 fusion.37
  9.6 4.4 %collective-permute-start = (bf16[1,17,1,64,256]{4,3,2,1,0:T(8,128)(2,1)}, bf16[1,17,1,64,256]{4,3,2,1,0:T(8,128)(2,1)}, u32[]{:S(2)}, u32[]{:S(2)}) collective-permute-start(bf16[1,17,1,64,256]{4,3,2,1,0:T(8,128)(2,1)} %get-tuple-element.12), channel_id=1, source_target_pairs={{0,1},{1,2},{2,3},{3,4},{4,5},{5,6},{6,7},{7,8},{8,9},{9,10},{10,1... | collective-permute-start | bytes 1671176 | tf_op jit(solution)/shard_map/ppermute | solution.py:15
  14.1 1.3 collective-permute-start.1
  15.4 2.8 fusion.26
  18.1 1.5 copy.8
  19.9 1.4 copy-done.3
  21.8 3.6 %collective-permute-done = bf16[1,17,1,64,256]{4,3,2,1,0:T(8,128)(2,1)} collective-permute-done((bf16[1,17,1,64,256]{4,3,2,1,0:T(8,128)(2,1)}, bf16[1,17,1,64,256]{4,3,2,1,0:T(8,128)(2,1)}, u32[]{:S(2)}, u32[]{:S(2)}) %collective-permute-start) | collective-permute-done | bytes 557088 | tf_op jit(solution)/shard_map/ppermute | solution.py:15
  25.4 4.9 %collective-permute-done.1 = bf16[1,17,1,64,256]{4,3,2,1,0:T(8,128)(2,1)} collective-permute-done((bf16[1,17,1,64,256]{4,3,2,1,0:T(8,128)(2,1)}, bf16[1,17,1,64,256]{4,3,2,1,0:T(8,128)(2,1)}, u32[]{:S(2)}, u32[]{:S(2)}) %collective-permute-start.1) | collective-permute-done | bytes 557088 | tf_op jit(solution)/shard_map/ppermute | solution.py:17
  30.4 1.5 maximum_bitcast_fusion
  35.7 2.9 multiply_convert_fusion
  39.1 1.8 fusion.28
  41.0 1.0 fusion.9
  42.0 4.4 %fusion.38 = f32[2304,256]{1,0:T(8,128)} fusion(bf16[2176,2304]{1,0:T(8,128)(2,1)S(1)} %bitcast.83, bf16[2176,256]{1,0:T(8,128)(2,1)S(1)} %fusion.9), kind=kOutput, calls=%fused_computation.75 | convolution fusion | flops 2566914048 | bytes 13500416 | tf_op jit(solution)/shard_map/dot_general | solution.py:101
  46.4 1.2 fusion.36
  47.6 3.5 %collective-permute-start.2 = (bf16[1,17,1,64,256]{4,3,2,1,0:T(8,128)(2,1)}, bf16[1,17,1,64,256]{4,3,2,1,0:T(8,128)(2,1)}, u32[]{:S(2)}, u32[]{:S(2)}) collective-permute-start(bf16[1,17,1,64,256]{4,3,2,1,0:T(8,128)(2,1)} %get-tuple-element.6), channel_id=1, source_target_pairs={{0,1},{1,2},{2,3},{3,4},{4,5},{5,6},{6,7},{7,8},{8,9},{9,10},{10,1... | collective-permute-start | bytes 1671176 | tf_op jit(solution)/shard_map/ppermute | solution.py:15
  51.2 1.3 collective-permute-start.3
  54.6 2.5 convolution_add_fusion.3
  57.1 2.5 fusion.4
  59.6 1.8 collective-permute-done.2
  61.4 4.9 %collective-permute-done.3 = bf16[1,17,1,64,256]{4,3,2,1,0:T(8,128)(2,1)} collective-permute-done((bf16[1,17,1,64,256]{4,3,2,1,0:T(8,128)(2,1)}, bf16[1,17,1,64,256]{4,3,2,1,0:T(8,128)(2,1)}, u32[]{:S(2)}, u32[]{:S(2)}) %collective-permute-start.3) | collective-permute-done | bytes 557088 | tf_op jit(solution)/shard_map/ppermute | solution.py:17
  66.3 1.5 maximum_bitcast_fusion.1
  72.3 3.8 %fusion = bf16[2176,256]{1,0:T(8,128)(2,1)} fusion(bf16[2176,2304]{1,0:T(8,128)(2,1)S(1)} %bitcast.84, bf16[2304,256]{1,0:T(8,128)(2,1)S(1)} %bitcast.79, bf16[2176,256]{1,0:T(8,128)(2,1)S(1)} %bitcast.67), kind=kOutput, calls=%fused_computation.5 | convolution fusion | flops 2568585216 | bytes 13434880 | tf_op jit(solution)/shard_map/dot_general | solution.py:91
  76.1 250.7 %all-reduce.7.cloned.1.call-done = (f32[2304,256]{1,0:T(8,128)}, f32[3,256,256]{2,1,0:T(8,128)}) async-done(((f32[2304,256]{1,0:T(8,128)}, f32[3,256,256]{2,1,0:T(8,128)}), (f32[2304,256]{1,0:T(8,128)}, f32[3,256,256]{2,1,0:T(8,128)})) %all-reduce.7.cloned.1.call-update) | async-done | bytes 3145744 | tf_op jit(solution)/shard_map/psum | solution.py:104
  326.8 3.3 broadcast_multiply_fusion
  (47 shorter events, 12.7 us)
Async XLA Ops:
  7.2 8.2 %copy-start = (bf16[1,17,2,64,256]{4,3,2,1,0:T(8,128)(2,1)S(1)}, bf16[1,17,2,64,256]{4,3,2,1,0:T(8,128)(2,1)}, u32[]{:S(2)}) copy-start(bf16[1,17,2,64,256]{4,3,2,1,0:T(8,128)(2,1)} %param.5) | copy-start | bytes 3342340
  7.2 319.6 %all-reduce.7.cloned.1.call-start = ((), (), s32[]{:S(2)}) async-start(), calls=%async_computation | async-start | bytes 6291456 | tf_op jit(solution)/shard_map/psum | solution.py:104
  9.6 8.5 %copy-start.6 = (bf16[3,3,256,256]{3,2,1,0:T(8,128)(2,1)S(1)}, bf16[3,3,256,256]{3,2,1,0:T(8,128)(2,1)}, u32[]{:S(2)}) copy-start(bf16[3,3,256,256]{3,2,1,0:T(8,128)(2,1)} %param.6) | copy-start | bytes 3538948
  9.6 15.8 %collective-permute-start = (bf16[1,17,1,64,256]{4,3,2,1,0:T(8,128)(2,1)}, bf16[1,17,1,64,256]{4,3,2,1,0:T(8,128)(2,1)}, u32[]{:S(2)}, u32[]{:S(2)}) collective-permute-start(bf16[1,17,1,64,256]{4,3,2,1,0:T(8,128)(2,1)} %get-tuple-element.12), channel_id=1, source_target_pairs={{0,1},{1,2},{2,3},{3,4},{4,5},{5,6},{6,7},{7,8},{8,9},{9,10},{10,1... | collective-permute-start | bytes 1671176 | tf_op jit(solution)/shard_map/ppermute | solution.py:15
  14.1 16.3 %collective-permute-start.1 = (bf16[1,17,1,64,256]{4,3,2,1,0:T(8,128)(2,1)}, bf16[1,17,1,64,256]{4,3,2,1,0:T(8,128)(2,1)}, u32[]{:S(2)}, u32[]{:S(2)}) collective-permute-start(bf16[1,17,1,64,256]{4,3,2,1,0:T(8,128)(2,1)} %get-tuple-element.13), channel_id=1, source_target_pairs={{1,0},{2,1},{3,2},{4,3},{5,4},{6,5},{7,6},{8,7},{9,8},{10,9},{11,1... | collective-permute-start | bytes 1671176 | tf_op jit(solution)/shard_map/ppermute | solution.py:17
  19.7 1.6 copy-start.3
  19.7 1.7 copy-start.8
  21.3 9.0 %copy-start.1 = (bf16[1,17,2,64,256]{4,3,2,1,0:T(8,128)(2,1)S(1)}, bf16[1,17,2,64,256]{4,3,2,1,0:T(8,128)(2,1)}, u32[]{:S(2)}) copy-start(bf16[1,17,2,64,256]{4,3,2,1,0:T(8,128)(2,1)} %param.4) | copy-start | bytes 3342340
  42.0 4.4 %copy-start.4 = (bf16[2176,256]{1,0:T(8,128)(2,1)}, bf16[2176,256]{1,0:T(8,128)(2,1)S(1)}, u32[]{:S(2)}) copy-start(bf16[2176,256]{1,0:T(8,128)(2,1)S(1)} %fusion.9) | copy-start | bytes 3342340
  47.6 13.7 %collective-permute-start.2 = (bf16[1,17,1,64,256]{4,3,2,1,0:T(8,128)(2,1)}, bf16[1,17,1,64,256]{4,3,2,1,0:T(8,128)(2,1)}, u32[]{:S(2)}, u32[]{:S(2)}) collective-permute-start(bf16[1,17,1,64,256]{4,3,2,1,0:T(8,128)(2,1)} %get-tuple-element.6), channel_id=1, source_target_pairs={{0,1},{1,2},{2,3},{3,4},{4,5},{5,6},{6,7},{7,8},{8,9},{9,10},{10,1... | collective-permute-start | bytes 1671176 | tf_op jit(solution)/shard_map/ppermute | solution.py:15
  51.2 15.1 %collective-permute-start.3 = (bf16[1,17,1,64,256]{4,3,2,1,0:T(8,128)(2,1)}, bf16[1,17,1,64,256]{4,3,2,1,0:T(8,128)(2,1)}, u32[]{:S(2)}, u32[]{:S(2)}) collective-permute-start(bf16[1,17,1,64,256]{4,3,2,1,0:T(8,128)(2,1)} %get-tuple-element.7), channel_id=1, source_target_pairs={{1,0},{2,1},{3,2},{4,3},{5,4},{6,5},{7,6},{8,7},{9,8},{10,9},{11,1... | collective-permute-start | bytes 1671176 | tf_op jit(solution)/shard_map/ppermute | solution.py:17
  52.6 1.0 copy-start.2
  57.1 9.2 %copy-start.5 = (bf16[2176,256]{1,0:T(8,128)(2,1)S(1)}, bf16[2176,256]{1,0:T(8,128)(2,1)}, u32[]{:S(2)}) copy-start(bf16[2176,256]{1,0:T(8,128)(2,1)} %copy-done.4) | copy-start | bytes 3342340
  71.0 1.3 copy-start.7
  326.8 3.4 copy-start.9
Sparse Core Ops, SparseCore 0:
  54.7 272.0 all-reduce.6
where the time goes:
time: 338 us
  waiting for transfers between devices  266 us (79%)
  matrix products  23.6 us (7%)
  local copies, waits for them, and re-layouts  15.4 us (5%)
  between operations  14.3 us (4%)
  starting transfers between devices  10.5 us (3%)
  other arithmetic  8.16 us (2%)
    psum x1, waiting for transfers between devices, body(): lax.psum((spatial_local, temporal_local), ('dp', 'tm'))  251 us
    unnamed x37, local copies, waits for them, and re-layouts  10.1 us
    ppermute x2, waiting for transfers between devices, with_halo(): lax.ppermute(head, axis, [((i + 1) % count, i) for i in range(ends)])  9.86 us
    ppermute x2, starting transfers between devices, with_halo(): lax.ppermute(tail, axis, [(i, (i + 1) % count) for i in range(ends)])  7.93 us
    dot_general x3, matrix products, causal_mix(): jnp.dot(earlier, weight[tap], preferred_element_type=jnp.float32)  6.79 us
  transfers between devices with their start and end apart: 5, of which 5 were waited for; matrix products, arithmetic and copies ran while one was open for 6% of the time, Pallas kernels for 0%

commit v1 on v0

--- a/solution.py
+++ b/solution.py
@@ -101,7 +101,7 @@
     spatial_local = lax.dot_general(
         patches, pre_grad, (((0,), (0,)), ((), ())), preferred_element_type=jnp.float32
     )
-    spatial_sum, temporal_sum = lax.psum((spatial_local, temporal_local), ("dp", "tm"))
+    spatial_sum, temporal_sum = lax.psum(lax.psum((spatial_local, temporal_local), "tm"), "dp")
     scale = (clips * lax.axis_size("dp") * frames * rows * lax.axis_size("tm") * cols) ** (-0.5)
     return (
         block_out.reshape(latents.shape),

time: 338 us -> 299 us (0.88)
  waiting for transfers between devices: 266 us -> 218 us
  local copies, waits for them, and re-layouts: 15.4 us -> 25.9 us
    psum x1 -> x2, waiting for transfers between devices: 251 us -> 190 us  [the longest x1 133 us: body(): lax.psum((spatial_local, temporal_local), 'tm')]
    ppermute x2, waiting for transfers between devices: 5.39 us -> 17.2 us  [with_halo(): lax.ppermute(tail, axis, [(i, (i + 1) % count) for i in range(ends)])]
    unnamed x37 -> x43, local copies, waits for them, and re-layouts: 10.1 us -> 20.1 us
    dot_general x3, matrix products: 6.79 us -> 2.38 us  [causal_mix(): jnp.dot(earlier, weight[tap], preferred_element_type=jnp.float32)]
    dot_general x1, matrix products: 3.77 us -> 7.62 us  [body(): jnp.dot(band_patches(grad_ext.reshape(clips * frames, rows + 2, cols, cha...]
  transfers between devices with their start and end apart: 5 -> 6, of which waited for: 5 -> 6; matrix products, arithmetic and copies ran while one was open for 6% -> 10% of each run, Pallas kernels for 0% -> 0%
where the time goes in v1:
time: 299 us; the launch traced here: 296 us
  waiting for transfers between devices  218 us (73%)
  local copies, waits for them, and re-layouts  25.9 us (9%)
  matrix products  21.7 us (7%)
  between operations  14.3 us (5%)
  starting transfers between devices  9.79 us (3%)
  other arithmetic  5.72 us (2%)
    psum x1, waiting for transfers between devices, body(): lax.psum((spatial_local, temporal_local), 'tm')  133 us
    psum x1, waiting for transfers between devices, body(): lax.psum(lax.psum((spatial_local, temporal_local), 'tm'), 'dp')  57.3 us
    unnamed x43, local copies, waits for them, and re-layouts  20.1 us
    ppermute x2, waiting for transfers between devices, with_halo(): lax.ppermute(tail, axis, [(i, (i + 1) % count) for i in range(ends)])  17.2 us
    ppermute x2, waiting for transfers between devices, with_halo(): lax.ppermute(head, axis, [((i + 1) % count, i) for i in range(ends)])  10.6 us
    dot_general x1, matrix products, body(): jnp.dot(band_patches(grad_ext.reshape(clips * frames, rows + 2, cols, cha...  7.62 us
    ppermute x2, starting transfers between devices, with_halo(): lax.ppermute(tail, axis, [(i, (i + 1) % count) for i in range(ends)])  7.13 us
  transfers between devices with their start and end apart: 6, of which 6 were waited for; matrix products, arithmetic and copies ran while one was open for 10% of the time, Pallas kernels for 0%

profile of v1, /device:TPU:2, one launch (start us, length us, event | category | flops | bytes accessed | tf_op | source)
XLA Modules:
  0.0 295.7 jit_solution(15650048487257457708)
XLA Ops:
  7.2 1.4 fusion.37
  8.6 3.5 %collective-permute-start = (bf16[1,17,1,64,256]{4,3,2,1,0:T(8,128)(2,1)S(1)}, bf16[1,17,1,64,256]{4,3,2,1,0:T(8,128)(2,1)S(1)}, u32[]{:S(2)}, u32[]{:S(2)}) collective-permute-start(bf16[1,17,1,64,256]{4,3,2,1,0:T(8,128)(2,1)S(1)} %get-tuple-element.14), channel_id=1, source_target_pairs={{0,1},{1,2},{2,3},{3,4},{4,5},{5,6},{6,7},{7,8},{8,9},{9,10},{10,1... | collective-permute-start | bytes 1671176 | tf_op jit(solution)/shard_map/ppermute | solution.py:15
  13.4 1.4 fusion.26
  16.4 7.6 %collective-permute-done = bf16[1,17,1,64,256]{4,3,2,1,0:T(8,128)(2,1)S(1)} collective-permute-done((bf16[1,17,1,64,256]{4,3,2,1,0:T(8,128)(2,1)S(1)}, bf16[1,17,1,64,256]{4,3,2,1,0:T(8,128)(2,1)S(1)}, u32[]{:S(2)}, u32[]{:S(2)}) %collective-permute-start) | collective-permute-done | bytes 557088 | tf_op jit(solution)/shard_map/ppermute | solution.py:15
  24.0 4.1 %collective-permute-done.1 = bf16[1,17,1,64,256]{4,3,2,1,0:T(8,128)(2,1)S(1)} collective-permute-done((bf16[1,17,1,64,256]{4,3,2,1,0:T(8,128)(2,1)S(1)}, bf16[1,17,1,64,256]{4,3,2,1,0:T(8,128)(2,1)S(1)}, u32[]{:S(2)}, u32[]{:S(2)}) %collective-permute-start.1) | collective-permute-done | bytes 557088 | tf_op jit(solution)/shard_map/ppermute | solution.py:17
  32.9 2.9 multiply_convert_fusion
  36.9 4.4 %fusion.38 = f32[2304,256]{1,0:T(8,128)} fusion(bf16[2176,2304]{1,0:T(8,128)(2,1)S(1)} %bitcast.83, bf16[2176,256]{1,0:T(8,128)(2,1)S(1)} %fusion.9), kind=kOutput, calls=%fused_computation.75 | convolution fusion | flops 2566914048 | bytes 13500416 | tf_op jit(solution)/shard_map/dot_general | solution.py:101
  44.5 2.4 copy.8
  47.0 1.3 fusion.36
  48.3 3.6 %collective-permute-start.2 = (bf16[1,17,1,64,256]{4,3,2,1,0:T(8,128)(2,1)S(1)}, bf16[1,17,1,64,256]{4,3,2,1,0:T(8,128)(2,1)S(1)}, u32[]{:S(2)}, u32[]{:S(2)}) collective-permute-start(bf16[1,17,1,64,256]{4,3,2,1,0:T(8,128)(2,1)S(1)} %get-tuple-element.8), channel_id=1, source_target_pairs={{0,1},{1,2},{2,3},{3,4},{4,5},{5,6},{6,7},{7,8},{8,9},{9,10},{10,1... | collective-permute-start | bytes 1671176 | tf_op jit(solution)/shard_map/ppermute | solution.py:15
  51.9 1.3 collective-permute-start.3
  55.0 1.5 fusion.4
  56.4 9.6 %collective-permute-done.2 = bf16[1,17,1,64,256]{4,3,2,1,0:T(8,128)(2,1)S(1)} collective-permute-done((bf16[1,17,1,64,256]{4,3,2,1,0:T(8,128)(2,1)S(1)}, bf16[1,17,1,64,256]{4,3,2,1,0:T(8,128)(2,1)S(1)}, u32[]{:S(2)}, u32[]{:S(2)}) %collective-permute-start.2) | collective-permute-done | bytes 557088 | tf_op jit(solution)/shard_map/ppermute | solution.py:15
  66.0 6.4 %collective-permute-done.3 = bf16[1,17,1,64,256]{4,3,2,1,0:T(8,128)(2,1)S(1)} collective-permute-done((bf16[1,17,1,64,256]{4,3,2,1,0:T(8,128)(2,1)S(1)}, bf16[1,17,1,64,256]{4,3,2,1,0:T(8,128)(2,1)S(1)}, u32[]{:S(2)}, u32[]{:S(2)}) %collective-permute-start.3) | collective-permute-done | bytes 557088 | tf_op jit(solution)/shard_map/ppermute | solution.py:17
  72.7 1.5 fusion.16
  75.3 1.8 fusion.17
  77.1 1.7 fusion.18
  79.9 133.1 %all-reduce.9.cloned.1.call-done = (f32[2304,256]{1,0:T(8,128)}, f32[3,256,256]{2,1,0:T(8,128)}) async-done(((f32[2304,256]{1,0:T(8,128)}, f32[3,256,256]{2,1,0:T(8,128)}), (f32[2304,256]{1,0:T(8,128)}, f32[3,256,256]{2,1,0:T(8,128)})) %all-reduce.9.cloned.1.call-update) | async-done | bytes 3145744 | tf_op jit(solution)/shard_map/psum | solution.py:104
  213.0 1.8 fusion.19
  214.8 1.8 fusion.20
  217.7 1.8 fusion.21
  219.6 7.6 %fusion = bf16[2176,256]{1,0:T(8,128)(2,1)} fusion(bf16[2176,2304]{1,0:T(8,128)(2,1)} %bitcast.17, bf16[2304,256]{1,0:T(8,128)(2,1)S(1)} %bitcast.79, bf16[2176,256]{1,0:T(8,128)(2,1)S(1)} %bitcast.67), kind=kOutput, calls=%fused_computation.5 | convolution fusion | flops 2568585216 | bytes 13434880 | tf_op jit(solution)/shard_map/dot_general | solution.py:91
  227.2 57.3 %all-reduce.11.cloned.1.call-done = (f32[2304,256]{1,0:T(8,128)}, f32[3,256,256]{2,1,0:T(8,128)}) async-done(((f32[2304,256]{1,0:T(8,128)}, f32[3,256,256]{2,1,0:T(8,128)}), (f32[2304,256]{1,0:T(8,128)}, f32[3,256,256]{2,1,0:T(8,128)})) %all-reduce.11.cloned.1.call-update) | async-done | bytes 3145744 | tf_op jit(solution)/shard_map/psum | solution.py:104
  284.5 3.3 %broadcast_multiply_fusion = f32[2304,256]{1,0:T(8,128)} fusion(f32[2304,256]{1,0:T(8,128)} %get-tuple-element.6), kind=kLoop, calls=%fused_computation.31 | loop fusion | flops 589824 | bytes 4718592 | tf_op jit(solution)/shard_map/mul | solution.py:109
  (56 shorter events, 18.2 us)
Async XLA Ops:
  7.2 6.3 %copy-start = (bf16[1,17,2,64,256]{4,3,2,1,0:T(8,128)(2,1)S(1)}, bf16[1,17,2,64,256]{4,3,2,1,0:T(8,128)(2,1)}, u32[]{:S(2)}) copy-start(bf16[1,17,2,64,256]{4,3,2,1,0:T(8,128)(2,1)} %param.5) | copy-start | bytes 3342340
  7.2 205.8 %all-reduce.9.cloned.1.call-start = ((), (), s32[]{:S(2)}) async-start(), calls=%async_computation | async-start | bytes 6291456 | tf_op jit(solution)/shard_map/psum | solution.py:104
  8.6 15.4 %collective-permute-start = (bf16[1,17,1,64,256]{4,3,2,1,0:T(8,128)(2,1)S(1)}, bf16[1,17,1,64,256]{4,3,2,1,0:T(8,128)(2,1)S(1)}, u32[]{:S(2)}, u32[]{:S(2)}) collective-permute-start(bf16[1,17,1,64,256]{4,3,2,1,0:T(8,128)(2,1)S(1)} %get-tuple-element.14), channel_id=1, source_target_pairs={{0,1},{1,2},{2,3},{3,4},{4,5},{5,6},{6,7},{7,8},{8,9},{9,10},{10,1... | collective-permute-start | bytes 1671176 | tf_op jit(solution)/shard_map/ppermute | solution.py:15
  12.1 16.0 %collective-permute-start.1 = (bf16[1,17,1,64,256]{4,3,2,1,0:T(8,128)(2,1)S(1)}, bf16[1,17,1,64,256]{4,3,2,1,0:T(8,128)(2,1)S(1)}, u32[]{:S(2)}, u32[]{:S(2)}) collective-permute-start(bf16[1,17,1,64,256]{4,3,2,1,0:T(8,128)(2,1)S(1)} %get-tuple-element.15), channel_id=1, source_target_pairs={{1,0},{2,1},{3,2},{4,3},{5,4},{6,5},{7,6},{8,7},{9,8},{10,9},{11,1... | collective-permute-start | bytes 1671176 | tf_op jit(solution)/shard_map/ppermute | solution.py:17
  14.8 1.0 copy-start.10
  15.8 12.3 %copy-start.1 = (bf16[1,17,2,64,256]{4,3,2,1,0:T(8,128)(2,1)S(1)}, bf16[1,17,2,64,256]{4,3,2,1,0:T(8,128)(2,1)}, u32[]{:S(2)}) copy-start(bf16[1,17,2,64,256]{4,3,2,1,0:T(8,128)(2,1)} %param.4) | copy-start | bytes 3342340
  31.6 1.3 copy-start.8
  36.8 4.4 %copy-start.6 = (bf16[2176,256]{1,0:T(8,128)(2,1)}, bf16[2176,256]{1,0:T(8,128)(2,1)S(1)}, u32[]{:S(2)}) copy-start(bf16[2176,256]{1,0:T(8,128)(2,1)S(1)} %fusion.9) | copy-start | bytes 3342340
  42.2 1.1 copy-start.2
  42.2 1.4 copy-start.4
  44.5 240.1 %all-reduce.11.cloned.1.call-start = ((), (), s32[]{:S(2)}) async-start(), calls=%async_computation.1 | async-start | bytes 6291456 | tf_op jit(solution)/shard_map/psum | solution.py:104
  47.0 6.3 %copy-start.11 = (bf16[3,256,256]{2,1,0:T(8,128)(2,1)S(1)}, bf16[3,256,256]{2,1,0:T(8,128)(2,1)}, u32[]{:S(2)}) copy-start(bf16[3,256,256]{2,1,0:T(8,128)(2,1)} %param.7) | copy-start | bytes 1179652
  48.3 5.4 %copy-start.5 = (bf16[1,17,128,256]{3,2,1,0:T(8,128)(2,1)S(1)}, bf16[1,17,128,256]{3,2,1,0:T(8,128)(2,1)}, u32[]{:S(2)}) copy-start(bf16[1,17,128,256]{3,2,1,0:T(8,128)(2,1)} %copy-done.4) | copy-start | bytes 3342340
  48.3 17.7 %collective-permute-start.2 = (bf16[1,17,1,64,256]{4,3,2,1,0:T(8,128)(2,1)S(1)}, bf16[1,17,1,64,256]{4,3,2,1,0:T(8,128)(2,1)S(1)}, u32[]{:S(2)}, u32[]{:S(2)}) collective-permute-start(bf16[1,17,1,64,256]{4,3,2,1,0:T(8,128)(2,1)S(1)} %get-tuple-element.8), channel_id=1, source_target_pairs={{0,1},{1,2},{2,3},{3,4},{4,5},{5,6},{6,7},{7,8},{8,9},{9,10},{10,1... | collective-permute-start | bytes 1671176 | tf_op jit(solution)/shard_map/ppermute | solution.py:15
  51.9 20.5 %collective-permute-start.3 = (bf16[1,17,1,64,256]{4,3,2,1,0:T(8,128)(2,1)S(1)}, bf16[1,17,1,64,256]{4,3,2,1,0:T(8,128)(2,1)S(1)}, u32[]{:S(2)}, u32[]{:S(2)}) collective-permute-start(bf16[1,17,1,64,256]{4,3,2,1,0:T(8,128)(2,1)S(1)} %get-tuple-element.9), channel_id=1, source_target_pairs={{1,0},{2,1},{3,2},{4,3},{5,4},{6,5},{7,6},{8,7},{9,8},{10,9},{11,1... | collective-permute-start | bytes 1671176 | tf_op jit(solution)/shard_map/ppermute | solution.py:17
  53.7 1.3 copy-start.3
  55.0 17.4 %copy-start.7 = (bf16[2176,256]{1,0:T(8,128)(2,1)S(1)}, bf16[2176,256]{1,0:T(8,128)(2,1)}, u32[]{:S(2)}) copy-start(bf16[2176,256]{1,0:T(8,128)(2,1)} %copy-done.6) | copy-start | bytes 3342340
  217.7 1.8 copy-start.9
  284.5 3.4 %copy-start.12 = (f32[3,256,256]{2,1,0:T(8,128)S(1)}, f32[3,256,256]{2,1,0:T(8,128)}, u32[]{:S(2)}) copy-start(f32[3,256,256]{2,1,0:T(8,128)} %get-tuple-element.7) | copy-start | bytes 2359300
Sparse Core Ops, SparseCore 0:
  44.6 168.3 all-reduce.8
  215.5 68.9 all-reduce.10
